TPU v7x, 32 devices: a whole 2x2x4 slice. The times are simulated.
32 devices in a mesh: fsdp: 8 (over z, x), ctx: 4 (over y, core).
Axes of the slice: x: 2, y: 2, z: 4, core: 2. Of those that a mesh axis runs over, the one named last changes fastest.
Arguments:
- tokens: bfloat16 [8, 512, 576], P('fsdp', 'ctx'), may hold values from -6 to 6
- positions: int32 [8, 512], P('fsdp'), may hold values from 0 to 511, as said below
- w_query: bfloat16 [576, 576], P('fsdp'), may hold values from -0.25 to 0.25
- w_key: bfloat16 [576, 192], P('fsdp'), may hold values from -0.25 to 0.25
- w_value: bfloat16 [576, 192], P('fsdp'), may hold values from -0.25 to 0.25
- w_output: bfloat16 [576, 576], P('fsdp'), may hold values from -2 to 2
- w_gate: bfloat16 [576, 1536], P('fsdp'), may hold values from -0.25 to 0.25
- w_up: bfloat16 [576, 1536], P('fsdp'), may hold values from -0.25 to 0.25
- w_down: bfloat16 [1536, 576], P('fsdp'), may hold values from -0.15625 to 0.15625
- gain_attention: bfloat16 [576], P('fsdp'), may hold values from 0.5 to 1.5
- gain_mlp: bfloat16 [576], P('fsdp'), may hold values from 0.5 to 1.5
- cotangent: bfloat16 [8, 512, 576], P('fsdp', 'ctx'), may hold values from -6 to 6
Outputs:
- block_out: bfloat16 [8, 512, 576], P('fsdp', 'ctx')
- grad_tokens: bfloat16 [8, 512, 576], P('fsdp', 'ctx')
- grad_w_query: float32 [576, 576], P('fsdp')
- grad_w_key: float32 [576, 192], P('fsdp')
- value_weight_gradient: float32 [576, 192], P('fsdp')
- grad_w_output: float32 [576, 576], P('fsdp')
- grad_w_gate: float32 [576, 1536], P('fsdp')
- grad_w_up: float32 [576, 1536], P('fsdp')
- grad_w_down: float32 [1536, 576], P('fsdp')
- grad_gain_attention: float32 [576], P('fsdp')
- grad_gain_mlp: float32 [576], P('fsdp')
Inputs may be any that keep to these rules, and one draw needn't show every extreme that they name: In each sequence the positions are a permutation of 0 to 511 made of aligned runs of 64 consecutive positions; the 128 rows that ctx gives one device are two such runs whose run numbers add to 7.
All inputs are finite; a program needn't handle non-finite values.
Results may differ from a plain program's by a relative error of at most 0.02.
Values may be sent and summed in bfloat16 or wider, within the bound.
No kernel may reach another device: no remote copies, remote signals or barrier semaphores. Data moves between devices by JAX's collectives and lax.ppermute only.
A program may use at most 128 MiB of HBM per device.

v0:
```python
import math
import jax
import jax.numpy as jnp
from jax import lax
from jax.sharding import PartitionSpec as P

HEADS = 9
KV_HEADS = 3
HEAD_DIM = 64
NORM_EPS = 1e-05
ROPE_BASE = 100000.0


def matmul(left, right):
    return jnp.dot(left, right, preferred_element_type=jnp.float32)


def rope_tables(position_rows):
    half_size = HEAD_DIM // 2
    frequency = ROPE_BASE ** (-jnp.arange(half_size, dtype=jnp.float32) / half_size)
    angles = position_rows.astype(jnp.float32)[:, None] * frequency[None, :]
    return (jnp.cos(angles)[:, None, :], jnp.sin(angles)[:, None, :])


def rotate(inputs, cos_table, sin_table, inverse):
    row_count = inputs.shape[0]
    halves = inputs.reshape(row_count, -1, 2, HEAD_DIM // 2)
    first_half = halves[:, :, 0]
    second_half = halves[:, :, 1]
    if inverse:
        new_first = first_half * cos_table + second_half * sin_table
        new_second = second_half * cos_table - first_half * sin_table
    else:
        new_first = first_half * cos_table - second_half * sin_table
        new_second = second_half * cos_table + first_half * sin_table
    return jnp.stack([new_first, new_second], axis=2).reshape(row_count, -1)


def norm_forward(inputs, gain):
    scale_row = lax.rsqrt(jnp.mean(inputs * inputs, axis=-1, keepdims=True) + NORM_EPS)
    return (scale_row, inputs * scale_row * gain.astype(jnp.float32))


def norm_backward(inputs, scale_row, gain, grad_normed):
    scaled_grad = grad_normed * gain.astype(jnp.float32)
    grad_gain = jnp.sum(grad_normed * inputs * scale_row, axis=0)
    inner_mean = jnp.mean(scaled_grad * inputs, axis=-1, keepdims=True)
    grad_inputs = scale_row * (scaled_grad - inputs * scale_row * scale_row * inner_mean)
    return (grad_inputs, grad_gain)


def slice_keys(kv_whole, seq_positions, first_row, key_rows):
    kv_width = KV_HEADS * HEAD_DIM
    kv_block = lax.dynamic_slice_in_dim(kv_whole, first_row, key_rows, 0)
    key_pos = lax.dynamic_slice_in_dim(seq_positions, first_row, key_rows, 0)
    key_block = kv_block[:, :kv_width].reshape(key_rows, KV_HEADS, HEAD_DIM)
    value_block = kv_block[:, kv_width:].reshape(key_rows, KV_HEADS, HEAD_DIM)
    return (key_block, value_block, key_pos)


def block_scores(query_heads, key_block, own_pos, key_pos):
    scores = jnp.einsum(
        "tgrd,kgd->grtk", query_heads, key_block, preferred_element_type=jnp.float32
    )
    visible = key_pos[None, :] <= own_pos[:, None]
    return (scores * HEAD_DIM ** (-0.5), visible)


def shards(
    tokens,
    positions,
    w_query,
    w_key,
    w_value,
    w_output,
    w_gate,
    w_up,
    w_down,
    gain_attention,
    gain_mlp,
    cotangent,
):
    single_precision = jnp.float32
    low = jnp.bfloat16
    row_count = tokens.shape[1]
    model_width = tokens.shape[2]
    group_size = HEADS // KV_HEADS
    kv_width = KV_HEADS * HEAD_DIM
    score_scale = HEAD_DIM ** (-0.5)
    x_float = tokens.reshape(row_count, model_width).astype(single_precision)
    cot_rows = cotangent.reshape(row_count, model_width)
    seq_positions = positions.reshape(-1)
    length = seq_positions.shape[0]
    own_pos = lax.dynamic_slice_in_dim(
        seq_positions, lax.axis_index("ctx") * row_count, row_count, 0
    )
    key_rows = math.gcd(length, 256)
    key_steps = length // key_rows
    gathered = (
        lax.all_gather(w_query, "fsdp", axis=0, tiled=True),
        lax.all_gather(w_key, "fsdp", axis=0, tiled=True),
        lax.all_gather(w_value, "fsdp", axis=0, tiled=True),
        lax.all_gather(w_output, "fsdp", axis=0, tiled=True),
        lax.all_gather(w_gate, "fsdp", axis=0, tiled=True),
        lax.all_gather(w_up, "fsdp", axis=0, tiled=True),
        lax.all_gather(w_down, "fsdp", axis=0, tiled=True),
        lax.all_gather(gain_attention, "fsdp", axis=0, tiled=True),
        lax.all_gather(gain_mlp, "fsdp", axis=0, tiled=True),
    )
    (
        query_full,
        key_full,
        value_full,
        output_full,
        gate_full,
        up_full,
        down_full,
        gain_first,
        gain_second,
    ) = gathered
    rms_first, normed = norm_forward(x_float, gain_first)
    normed_first = normed.astype(low)
    cos_table, sin_table = rope_tables(own_pos)
    queries = rotate(matmul(normed_first, query_full), cos_table, sin_table, False).astype(low)
    keys = rotate(matmul(normed_first, key_full), cos_table, sin_table, False).astype(low)
    values = matmul(normed_first, value_full).astype(low)
    local_kv = jnp.concatenate([keys, values], axis=1)
    kv_whole = lax.all_gather(local_kv, "ctx", axis=0, tiled=True)
    query_heads = queries.reshape(row_count, KV_HEADS, group_size, HEAD_DIM)

    def add_totals(index, totals):
        key_block, value_block, key_pos = slice_keys(
            kv_whole, seq_positions, index * key_rows, key_rows
        )
        scores, visible = block_scores(query_heads, key_block, own_pos, key_pos)
        return totals + jnp.sum(jnp.where(visible, jnp.exp(scores), 0.0), axis=-1)

    totals = lax.fori_loop(
        0, key_steps, add_totals, jnp.zeros((KV_HEADS, group_size, row_count), single_precision)
    )
    logsum = jnp.log(totals)

    def add_output(index, running):
        key_block, value_block, key_pos = slice_keys(
            kv_whole, seq_positions, index * key_rows, key_rows
        )
        scores, visible = block_scores(query_heads, key_block, own_pos, key_pos)
        probs = jnp.where(visible, jnp.exp(scores - logsum[..., None]), 0.0).astype(low)
        return running + jnp.einsum(
            "grtk,kgd->tgrd", probs, value_block, preferred_element_type=single_precision
        )

    mixed = lax.fori_loop(
        0,
        key_steps,
        add_output,
        jnp.zeros((row_count, KV_HEADS, group_size, HEAD_DIM), single_precision),
    )
    attended = mixed.reshape(row_count, model_width).astype(low)
    residual = x_float + matmul(attended, output_full)
    rms_second, normed = norm_forward(residual, gain_second)
    normed_second = normed.astype(low)
    gate_values = matmul(normed_second, gate_full)
    up_values = matmul(normed_second, up_full)
    sigmoid_gate = jax.nn.sigmoid(gate_values)
    middle = (gate_values * sigmoid_gate * up_values).astype(low)
    block_out = (residual + matmul(middle, down_full)).astype(low)
    regathered = (
        lax.all_gather(w_query, "fsdp", axis=0, tiled=True),
        lax.all_gather(w_key, "fsdp", axis=0, tiled=True),
        lax.all_gather(w_value, "fsdp", axis=0, tiled=True),
        lax.all_gather(w_output, "fsdp", axis=0, tiled=True),
        lax.all_gather(w_gate, "fsdp", axis=0, tiled=True),
        lax.all_gather(w_up, "fsdp", axis=0, tiled=True),
        lax.all_gather(w_down, "fsdp", axis=0, tiled=True),
        lax.all_gather(gain_attention, "fsdp", axis=0, tiled=True),
        lax.all_gather(gain_mlp, "fsdp", axis=0, tiled=True),
    )
    (
        query_back_w,
        key_back_w,
        value_back_w,
        output_back_w,
        gate_back_w,
        up_back_w,
        down_back_w,
        gain_first_b,
        gain_second_b,
    ) = regathered
    kv_back = lax.all_gather(local_kv, "ctx", axis=0, tiled=True)
    grad_down = matmul(middle.T, cot_rows)
    grad_middle = matmul(cot_rows, down_back_w.T)
    grad_gate = (
        grad_middle * up_values * sigmoid_gate * (1.0 + gate_values * (1.0 - sigmoid_gate))
    ).astype(low)
    grad_up_low = (grad_middle * gate_values * sigmoid_gate).astype(low)
    grad_gate_w = matmul(normed_second.T, grad_gate)
    grad_up_w = matmul(normed_second.T, grad_up_low)
    grad_normed_second = matmul(grad_gate, gate_back_w.T) + matmul(grad_up_low, up_back_w.T)
    grad_resid_norm, grad_gain_mlp = norm_backward(
        residual, rms_second, gain_second_b, grad_normed_second
    )
    grad_residual = cot_rows.astype(single_precision) + grad_resid_norm
    grad_residual_low = grad_residual.astype(low)
    grad_output_w = matmul(attended.T, grad_residual_low)
    grad_attended = matmul(grad_residual_low, output_back_w.T).astype(low)
    attention_head_gradient = grad_attended.reshape(row_count, KV_HEADS, group_size, HEAD_DIM)
    attention_head_rows = attended.reshape(row_count, KV_HEADS, group_size, HEAD_DIM)
    row_correction = jnp.einsum(
        "kzwn->zwk",
        attention_head_gradient.astype(single_precision)
        * attention_head_rows.astype(single_precision),
    )

    def score_grads(key_block, value_block, key_pos):
        scores, visible = block_scores(query_heads, key_block, own_pos, key_pos)
        soft = jnp.where(visible, jnp.exp(scores - logsum[..., None]), 0.0)
        grad_soft = jnp.einsum(
            "tgrd,kgd->grtk",
            attention_head_gradient,
            value_block,
            preferred_element_type=single_precision,
        )
        grad_scores = (soft * (grad_soft - row_correction[..., None]) * score_scale).astype(low)
        return (soft, grad_scores)

    def add_query_grad(index, running):
        key_block, value_block, key_pos = slice_keys(
            kv_back, seq_positions, index * key_rows, key_rows
        )
        soft, grad_scores = score_grads(key_block, value_block, key_pos)
        return running + jnp.einsum(
            "grtk,kgd->tgrd", grad_scores, key_block, preferred_element_type=single_precision
        )

    grad_query_heads = lax.fori_loop(
        0,
        key_steps,
        add_query_grad,
        jnp.zeros((row_count, KV_HEADS, group_size, HEAD_DIM), single_precision),
    )
    sub_rows = math.gcd(row_count * lax.axis_size("ctx"), key_rows)

    def one_piece(piece_index):
        key_block, value_block, key_pos = slice_keys(
            kv_back, seq_positions, piece_index * sub_rows, sub_rows
        )
        soft, grad_scores = score_grads(key_block, value_block, key_pos)
        key_grad = jnp.einsum(
            "grtk,tgrd->kgd", grad_scores, query_heads, preferred_element_type=single_precision
        )
        value_grad = jnp.einsum(
            "grtk,tgrd->kgd",
            soft.astype(low),
            attention_head_gradient,
            preferred_element_type=single_precision,
        )
        return jnp.concatenate(
            [key_grad.reshape(sub_rows, kv_width), value_grad.reshape(sub_rows, kv_width)], axis=1
        )

    pieces = lax.map(
        one_piece, jnp.arange(row_count * lax.axis_size("ctx") // sub_rows, dtype=jnp.int32)
    )
    kv_grads = lax.psum_scatter(
        pieces.reshape(row_count * lax.axis_size("ctx"), 2 * kv_width).astype(jnp.bfloat16),
        "ctx",
        scatter_dimension=0,
        tiled=True,
    ).astype(jnp.float32)
    query_back = rotate(
        grad_query_heads.reshape(row_count, model_width), cos_table, sin_table, True
    ).astype(low)
    key_back = rotate(kv_grads[:, :kv_width], cos_table, sin_table, True).astype(low)
    value_back = kv_grads[:, kv_width:].astype(low)
    grad_query_w = matmul(normed_first.T, query_back)
    grad_key_w = matmul(normed_first.T, key_back)
    grad_value_w = matmul(normed_first.T, value_back)
    grad_normed_first = (
        matmul(query_back, query_back_w.T)
        + matmul(key_back, key_back_w.T)
        + matmul(value_back, value_back_w.T)
    )
    grad_tok_norm, grad_gain_attention = norm_backward(
        x_float, rms_first, gain_first_b, grad_normed_first
    )
    grad_tokens = (grad_residual + grad_tok_norm).astype(low)
    owned = (
        lax.psum_scatter(
            grad_query_w.astype(jnp.bfloat16), "fsdp", scatter_dimension=0, tiled=True
        ).astype(jnp.float32),
        lax.psum_scatter(
            grad_key_w.astype(jnp.bfloat16), "fsdp", scatter_dimension=0, tiled=True
        ).astype(jnp.float32),
        lax.psum_scatter(
            grad_value_w.astype(jnp.bfloat16), "fsdp", scatter_dimension=0, tiled=True
        ).astype(jnp.float32),
        lax.psum_scatter(
            grad_output_w.astype(jnp.bfloat16), "fsdp", scatter_dimension=0, tiled=True
        ).astype(jnp.float32),
        lax.psum_scatter(
            grad_gate_w.astype(jnp.bfloat16), "fsdp", scatter_dimension=0, tiled=True
        ).astype(jnp.float32),
        lax.psum_scatter(
            grad_up_w.astype(jnp.bfloat16), "fsdp", scatter_dimension=0, tiled=True
        ).astype(jnp.float32),
        lax.psum_scatter(
            grad_down.astype(jnp.bfloat16), "fsdp", scatter_dimension=0, tiled=True
        ).astype(jnp.float32),
        lax.psum_scatter(
            grad_gain_attention.astype(jnp.bfloat16), "fsdp", scatter_dimension=0, tiled=True
        ).astype(jnp.float32),
        lax.psum_scatter(
            grad_gain_mlp.astype(jnp.bfloat16), "fsdp", scatter_dimension=0, tiled=True
        ).astype(jnp.float32),
    )
    summed = (
        lax.psum(owned[0].astype(jnp.bfloat16), "ctx").astype(jnp.float32),
        lax.psum(owned[1].astype(jnp.bfloat16), "ctx").astype(jnp.float32),
        lax.psum(owned[2].astype(jnp.bfloat16), "ctx").astype(jnp.float32),
        lax.psum(owned[3].astype(jnp.bfloat16), "ctx").astype(jnp.float32),
        lax.psum(owned[4].astype(jnp.bfloat16), "ctx").astype(jnp.float32),
        lax.psum(owned[5].astype(jnp.bfloat16), "ctx").astype(jnp.float32),
        lax.psum(owned[6].astype(jnp.bfloat16), "ctx").astype(jnp.float32),
        lax.psum(owned[7].astype(jnp.bfloat16), "ctx").astype(jnp.float32),
        lax.psum(owned[8].astype(jnp.bfloat16), "ctx").astype(jnp.float32),
    )
    return (
        block_out.reshape(1, row_count, model_width),
        grad_tokens.reshape(1, row_count, model_width),
        summed[0],
        summed[1],
        summed[2],
        summed[3],
        summed[4],
        summed[5],
        summed[6],
        summed[7],
        summed[8],
    )


def solution(mesh):
    return jax.shard_map(
        shards,
        mesh=mesh,
        in_specs=(
            P("fsdp", "ctx", None),
            P("fsdp", None),
            P("fsdp", None),
            P("fsdp", None),
            P("fsdp", None),
            P("fsdp", None),
            P("fsdp", None),
            P("fsdp", None),
            P("fsdp", None),
            P("fsdp"),
            P("fsdp"),
            P("fsdp", "ctx", None),
        ),
        out_specs=(
            P("fsdp", "ctx", None),
            P("fsdp", "ctx", None),
            P("fsdp", None),
            P("fsdp", None),
            P("fsdp", None),
            P("fsdp", None),
            P("fsdp", None),
            P("fsdp", None),
            P("fsdp", None),
            P("fsdp"),
            P("fsdp"),
        ),
        check_vma=False,
    )
```

profile of v0, /device:TPU:0, one launch (start us, length us, event | category | flops | bytes accessed | tf_op | source)
XLA Modules:
  0.0 731.1 jit_solution(7201682807564454991)
XLA Ops:
  13.2 23.4 %all-reduce.7 = (bf16[576]{0:T(1024)(128)(2,1)S(1)}, bf16[576]{0:T(1024)(128)(2,1)S(1)}) all-reduce(bf16[576]{0:T(1024)(128)(2,1)S(1)} %dynamic-update-slice, bf16[576]{0:T(1024)(128)(2,1)S(1)} %dynamic-update-slice.1), channel_id=1, replica_groups=mesh['fsdp'=8,'ctx'=4] {'fsdp'}, use_global_device_ids=true, to_apply=%add | all-reduce | flops 1152 | bytes 4608
  37.6 31.9 %all_gather.41 = bf16[576,192]{1,0:T(8,128)(2,1)S(1)} all-gather(bf16[72,192]{1,0:T(8,128)(2,1)} %param.23), channel_id=1, replica_groups=mesh['fsdp'=8,'ctx'=4] {'fsdp'}, dimensions={0}, use_global_device_ids=true | all-gather | bytes 248832 | tf_op jit(solution)/shard_map/all_gather | solution.py:101
  69.7 31.9 %all_gather.42 = bf16[576,192]{1,0:T(8,128)(2,1)S(1)} all-gather(bf16[72,192]{1,0:T(8,128)(2,1)S(1)} %copy-done.44), channel_id=1, replica_groups=mesh['fsdp'=8,'ctx'=4] {'fsdp'}, dimensions={0}, use_global_device_ids=true | all-gather | bytes 248832 | tf_op jit(solution)/shard_map/all_gather | solution.py:102
  102.6 6.4 all_gather.43
  109.1 32.5 %all_gather.44 = bf16[576,576]{1,0:T(8,128)(2,1)S(1)} all-gather(bf16[72,576]{1,0:T(8,128)(2,1)S(1)} %copy-done.40), channel_id=1, replica_groups=mesh['fsdp'=8,'ctx'=4] {'fsdp'}, dimensions={0}, use_global_device_ids=true | all-gather | bytes 746496 | tf_op jit(solution)/shard_map/all_gather | solution.py:100
  145.8 33.6 %all_gather.45 = bf16[576,576]{1,0:T(8,128)(2,1)S(1)} all-gather(bf16[72,576]{1,0:T(8,128)(2,1)S(1)} %copy-done.41), channel_id=1, replica_groups=mesh['fsdp'=8,'ctx'=4] {'fsdp'}, dimensions={0}, use_global_device_ids=true | all-gather | bytes 746496 | tf_op jit(solution)/shard_map/all_gather | solution.py:103
  180.0 2.9 fusion.90
  182.9 2.9 fusion.91
  185.8 3.8 multiply_convert_fusion
  193.7 8.5 %while.52 = (s32[]{:T(128)}, bf16[2,256,384]{2,1,0:T(8,128)(2,1)}, s32[2]{0:T(128)S(1)}, s32[512]{0:T(512)S(1)}, s32[128]{0:T(128)S(1)}, /*index=5*/bf16[512,384...) while((s32[]{:T(128)}, bf16[2,256,384]{2,1,0:T(8,128)(2,1)}, ...), condition=%wide.region_12.13_spmd, body=%wide.region_11.12_spmd.sunk | while | flops 153780224 | bytes 9319195 | solution.py:262
  202.2 2.2 convolution_convert_fusion.3
  204.5 2.4 while.55
  209.1 1.8 convolution_convert_fusion.2
  214.8 2.0 convolution_convert_fusion
  225.8 21.5 %all-reduce.6 = (bf16[576]{0:T(1024)(128)(2,1)S(1)}, bf16[576]{0:T(1024)(128)(2,1)S(1)}) all-reduce(bf16[576]{0:T(1024)(128)(2,1)S(1)} %get-tuple-element.563, bf16[576]{0:T(1024)(128)(2,1)S(1)} %copy-done.48), channel_id=10, replica_groups=mesh['fsdp'=8,'ctx'=4] {'fsdp'}, use_global_device_ids=true, to_apply=%region_30.31.clone | all-reduce | flops 1152 | bytes 4608
  247.5 37.4 %reduce-scatter.29.cloned.1.call-done = bf16[72,576]{1,0:T(8,128)(2,1)} async-done(((bf16[576,576]{1,0:T(8,128)(2,1)}), bf16[72,576]{1,0:T(8,128)(2,1)}) %reduce-scatter.29.cloned.1.call-update) | async-done | bytes 82960
  284.9 63.5 %reduce-scatter.27.cloned.1.call-done = bf16[72,576]{1,0:T(8,128)(2,1)} async-done(((bf16[576,576]{1,0:T(8,128)(2,1)}), bf16[72,576]{1,0:T(8,128)(2,1)}) %reduce-scatter.27.cloned.1.call-update) | async-done | bytes 82960
  348.4 69.0 %reduce-scatter.19.cloned.1.call-done = bf16[72,1536]{1,0:T(8,128)(2,1)} async-done(((bf16[576,1536]{1,0:T(8,128)(2,1)}), bf16[72,1536]{1,0:T(8,128)(2,1)}) %reduce-scatter.19.cloned.1.call-update) | async-done | bytes 221200 | tf_op jit(solution)/shard_map/reduce_scatter | solution.py:301
  417.4 69.0 %reduce-scatter.21.cloned.1.call-done = bf16[72,1536]{1,0:T(8,128)(2,1)} async-done(((bf16[576,1536]{1,0:T(8,128)(2,1)}), bf16[72,1536]{1,0:T(8,128)(2,1)}) %reduce-scatter.21.cloned.1.call-update) | async-done | bytes 221200 | tf_op jit(solution)/shard_map/reduce_scatter | solution.py:304
  486.5 69.8 %reduce-scatter.23.cloned.1.call-done = bf16[192,576]{1,0:T(8,128)(2,1)} async-done(((bf16[1536,576]{1,0:T(8,128)(2,1)}), bf16[192,576]{1,0:T(8,128)(2,1)}) %reduce-scatter.23.cloned.1.call-update) | async-done | bytes 221200 | tf_op jit(solution)/shard_map/reduce_scatter | solution.py:307
  557.1 61.4 %reduce-scatter.15.cloned.1.call-done = bf16[72,192]{1,0:T(8,128)(2,1)} async-done(((bf16[576,192]{1,0:T(8,128)(2,1)}), bf16[72,192]{1,0:T(8,128)(2,1)}) %reduce-scatter.15.cloned.1.call-update) | async-done | bytes 27664 | tf_op jit(solution)/shard_map/reduce_scatter | solution.py:292
  618.4 62.5 %reduce-scatter.17.cloned.1.call-done = bf16[72,192]{1,0:T(8,128)(2,1)} async-done(((bf16[576,192]{1,0:T(8,128)(2,1)}), bf16[72,192]{1,0:T(8,128)(2,1)}) %reduce-scatter.17.cloned.1.call-update) | async-done | bytes 27664 | tf_op jit(solution)/shard_map/reduce_scatter | solution.py:295
  680.9 12.2 %all-reduce.8 = (bf16[72,192]{1,0:T(8,128)(2,1)S(1)}, bf16[72,192]{1,0:T(8,128)(2,1)S(1)}, bf16[72]{0:T(256)(128)(2,1)S(1)}, bf16[72]{0:T(256)(128)(2,1)S(1)}) all-reduce(bf16[72,192]{1,0:T(8,128)(2,1)} %reduce-scatter.15.cloned.1.call-done, ...), channel_id=1, replica_groups=mesh['fsdp'=8,'ctx'=4] {'ctx'}, use_global_device_ids=true, to_apply=%region_18.19 | all-reduce | flops 27792 | bytes 111168 | tf_op jit(solution)/shard_map/psum | solution.py:319
  695.4 23.1 %all-reduce.12.cloned.1.call-done = (bf16[72,576]{1,0:T(8,128)(2,1)}, bf16[72,576]{1,0:T(8,128)(2,1)}, bf16[72,1536]{1,0:T(8,128)(2,1)}, bf16[72,1536]{1,0:T(8,128)(2,1)}, bf16[192,576]{1,0:T(8,128)(2,1)}) async-done(((bf16[72,576]{1,0:T(8,128)(2,1)}, bf16[72,576]{1,0:T(8,128)(2,1)}, bf16[72,1536]{1,0:T(8,128)(2,1)}, bf16[72,1536]{1,0:T(8,128)(2,1)}, bf16[192,576]{1,0:T(8,128)(2,1)}), ...) | async-done | bytes 829456 | tf_op jit(solution)/shard_map/psum | solution.py:318
  (246 shorter events, 51.5 us)
Async XLA Ops:
  7.2 94.4 %copy-start = (bf16[1,128,576]{1,2,0:T(8,128)(2,1)S(1)}, bf16[1,128,576]{1,2,0:T(8,128)(2,1)}, u32[]{:S(2)}) copy-start(bf16[1,128,576]{1,2,0:T(8,128)(2,1)} %param.20) | copy-start | bytes 442372
  7.2 62.5 %copy-start.44 = (bf16[72,192]{1,0:T(8,128)(2,1)S(1)}, bf16[72,192]{1,0:T(8,128)(2,1)}, u32[]{:S(2)}) copy-start(bf16[72,192]{1,0:T(8,128)(2,1)} %param.24) | copy-start | bytes 82948
  7.2 172.8 %all-gather.4.cloned.1.call-start = ((), (), s32[]{:S(2)}) async-start(), calls=%async_computation.8 | async-start | bytes 1990656 | tf_op jit(solution)/shard_map/all_gather | solution.py:104
  7.9 175.0 %all-gather.6.cloned.1.call-start = ((), (), s32[]{:S(2)}) async-start(), calls=%async_computation.9 | async-start | bytes 1990656 | tf_op jit(solution)/shard_map/all_gather | solution.py:105
  8.7 177.1 %all-gather.8.cloned.1.call-start = ((), (), s32[]{:S(2)}) async-start(), calls=%async_computation.10 | async-start | bytes 2211840 | tf_op jit(solution)/shard_map/all_gather | solution.py:106
  9.4 210.9 %reduce-scatter.25.cloned.1.call-start = ((), (), s32[]{:S(2)}) async-start(), calls=%async_computation.16 | async-start | bytes 491520
  36.6 170.5 %copy-start.37 = (f32[576]{0:T(1024)}, f32[576]{0:T(1024)S(1)}, u32[]{:S(2)}) copy-start(f32[576]{0:T(1024)S(1)} %convert_element_type.219) | copy-start | bytes 6916
  36.6 65.8 %copy-start.36 = (s32[1,512]{1,0:T(1,128)S(1)}, s32[1,512]{1,0:T(1,128)}, u32[]{:S(2)}) copy-start(s32[1,512]{1,0:T(1,128)} %param.21) | copy-start | bytes 6148
  37.6 169.5 %copy-start.45 = (f32[128]{0:T(128)}, f32[128]{0:T(128)S(1)}, u32[]{:S(2)}) copy-start(f32[128]{0:T(128)S(1)} %add_rsqrt_fusion.1) | copy-start | bytes 1540
  69.5 33.1 %copy-start.9 = (bf16[576,192]{1,0:T(8,128)(2,1)}, bf16[576,192]{1,0:T(8,128)(2,1)S(1)}, u32[]{:S(2)}) copy-start(bf16[576,192]{1,0:T(8,128)(2,1)S(1)} %all_gather.41) | copy-start | bytes 663556
  69.7 39.3 %copy-start.40 = (bf16[72,576]{1,0:T(8,128)(2,1)S(1)}, bf16[72,576]{1,0:T(8,128)(2,1)}, u32[]{:S(2)}) copy-start(bf16[72,576]{1,0:T(8,128)(2,1)} %param.22) | copy-start | bytes 248836
  102.5 104.4 %copy-start.29 = (f32[128,32]{0,1:T(8,128)}, f32[128,32]{0,1:T(8,128)S(1)}, u32[]{:S(2)}) copy-start(f32[128,32]{0,1:T(8,128)S(1)} %get-tuple-element.662) | copy-start | bytes 49156
  145.7 34.1 %copy-start.25 = (f32[128,3,3,64]{0,3,2,1:T(8,128)}, f32[128,3,3,64]{0,3,2,1:T(8,128)S(1)}, u32[]{:S(2)}) copy-start(f32[128,3,3,64]{0,3,2,1:T(8,128)S(1)} %get-tuple-element.451) | copy-start | bytes 884740
  145.7 34.1 %copy-start.18 = (bf16[128,3,3,64]{0,3,2,1:T(8,128)(2,1)}, bf16[128,3,3,64]{0,3,2,1:T(8,128)(2,1)S(1)}, u32[]{:S(2)}) copy-start(bf16[128,3,3,64]{0,3,2,1:T(8,128)(2,1)S(1)} %convert_element_type.227) | copy-start | bytes 442372
  193.6 8.6 %copy-start.19 = (bf16[128,3,3,64]{0,3,2,1:T(8,128)(2,1)S(1)}, bf16[128,3,3,64]{0,3,2,1:T(8,128)(2,1)}, u32[]{:S(2)}) copy-start(bf16[128,3,3,64]{0,3,2,1:T(8,128)(2,1)} %copy-done.18) | copy-start | bytes 442372
  202.1 82.7 %reduce-scatter.29.cloned.1.call-start = ((), (), s32[]{:S(2)}) async-start(), calls=%async_computation.18 | async-start | bytes 829440
  204.5 144.0 %reduce-scatter.27.cloned.1.call-start = ((), (), s32[]{:S(2)}) async-start(), calls=%async_computation.17 | async-start | bytes 829440
  209.0 208.4 %reduce-scatter.19.cloned.1.call-start = ((), (), s32[]{:S(2)}) async-start(), calls=%async_computation.13 | async-start | bytes 1990656 | tf_op jit(solution)/shard_map/reduce_scatter | solution.py:301
  211.0 275.5 %reduce-scatter.21.cloned.1.call-start = ((), (), s32[]{:S(2)}) async-start(), calls=%async_computation.14 | async-start | bytes 1990656 | tf_op jit(solution)/shard_map/reduce_scatter | solution.py:304
  213.8 342.4 %reduce-scatter.23.cloned.1.call-start = ((), (), s32[]{:S(2)}) async-start(), calls=%async_computation.15 | async-start | bytes 2211840 | tf_op jit(solution)/shard_map/reduce_scatter | solution.py:307
  216.8 401.6 %reduce-scatter.15.cloned.1.call-start = ((), (), s32[]{:S(2)}) async-start(), calls=%async_computation.11 | async-start | bytes 331776 | tf_op jit(solution)/shard_map/reduce_scatter | solution.py:292
  222.4 458.5 %reduce-scatter.17.cloned.1.call-start = ((), (), s32[]{:S(2)}) async-start(), calls=%async_computation.12 | async-start | bytes 331776 | tf_op jit(solution)/shard_map/reduce_scatter | solution.py:295
  225.0 493.5 %all-reduce.12.cloned.1.call-start = ((), (), s32[]{:S(2)}) async-start(), calls=%async_computation.19 | async-start | bytes 1744896 | tf_op jit(solution)/shard_map/psum | solution.py:318
  225.3 330.9 %copy-start.6 = (f32[128,576]{0,1:T(8,128)S(1)}, f32[128,576]{0,1:T(8,128)}, u32[]{:S(2)}) copy-start(f32[128,576]{0,1:T(8,128)} %copy-done.5) | copy-start | bytes 884740
  (39 other events, 78.8 us)
Sparse Core Ops, SparseCore 0:
  10.2 51.9 all-gather.3
  64.3 47.1 all-gather.5
  113.7 56.9 all-gather.7
  202.3 17.9 reduce-scatter.24
  223.5 61.3 reduce-scatter.28
  288.1 60.2 reduce-scatter.26
  351.9 65.4 reduce-scatter.18
  420.9 65.5 reduce-scatter.20
  489.9 66.2 reduce-scatter.22
  559.9 58.4 reduce-scatter.14
  622.3 58.5 reduce-scatter.16
  683.5 34.9 all-reduce.11
where the time goes:
time: 732 us; the launch traced here: 731 us
  waiting for transfers between devices  459 us (63%)
  blocking collectives  193 us (26%)
  matrix products  34.3 us (5%)
  between operations  16.3 us (2%)
  local copies, waits for them, and re-layouts  14 us (2%)
  other arithmetic  11.5 us (2%)
    unnamed x15, waiting for transfers between devices  104 us
    reduce_scatter x1, waiting for transfers between devices, shards(): lax.psum_scatter(grad_down.astype(jnp.bfloat16), 'fsdp', scatter_dimensio...  69.8 us
    reduce_scatter x1, waiting for transfers between devices, shards(): lax.psum_scatter(grad_up_w.astype(jnp.bfloat16), 'fsdp', scatter_dimensio...  69 us
    reduce_scatter x1, waiting for transfers between devices, shards(): lax.psum_scatter(grad_gate_w.astype(jnp.bfloat16), 'fsdp', scatter_dimens...  69 us
    reduce_scatter x1, waiting for transfers between devices, shards(): lax.psum_scatter(grad_value_w.astype(jnp.bfloat16), 'fsdp', scatter_dimen...  62.5 us
    reduce_scatter x1, waiting for transfers between devices, shards(): lax.psum_scatter(grad_key_w.astype(jnp.bfloat16), 'fsdp', scatter_dimensi...  61.4 us
    unnamed x2, blocking collectives  44.8 us
    all_gather x1, blocking collectives, shards(): lax.all_gather(w_output, 'fsdp', axis=0, tiled=True)  33.6 us
  transfers between devices with their start and end apart: 12, of which 9 were waited for; matrix products, arithmetic and copies ran while one was open for 5% of the time, Pallas kernels for 0%

commit v1 on v0

--- a/solution.py
+++ b/solution.py
@@ -315,7 +315,9 @@
         ).astype(jnp.float32),
     )
     summed = (
-        lax.psum(owned[0].astype(jnp.bfloat16), "ctx").astype(jnp.float32),
+        jnp.sum(lax.all_gather(owned[0].astype(jnp.bfloat16), axis_name="ctx"), axis=0).astype(
+            jnp.float32
+        ),
         lax.psum(owned[1].astype(jnp.bfloat16), "ctx").astype(jnp.float32),
         lax.psum(owned[2].astype(jnp.bfloat16), "ctx").astype(jnp.float32),
         lax.psum(owned[3].astype(jnp.bfloat16), "ctx").astype(jnp.float32),

time: 732 us -> 729 us (level)
    unnamed x15, waiting for transfers between devices: 104 us -> 92.2 us
where the time goes in v1:
time: 729 us; the launch traced here: 728 us
  waiting for transfers between devices  453 us (62%)
  blocking collectives  199 us (27%)
  matrix products  33.2 us (5%)
  between operations  16.1 us (2%)
  local copies, waits for them, and re-layouts  13.3 us (2%)
  other arithmetic  11.5 us (2%)
    unnamed x15, waiting for transfers between devices  92.2 us
    reduce_scatter x1, waiting for transfers between devices, shards(): lax.psum_scatter(grad_down.astype(jnp.bfloat16), 'fsdp', scatter_dimensio...  69.8 us
    reduce_scatter x1, waiting for transfers between devices, shards(): lax.psum_scatter(grad_up_w.astype(jnp.bfloat16), 'fsdp', scatter_dimensio...  69 us
    reduce_scatter x1, waiting for transfers between devices, shards(): lax.psum_scatter(grad_gate_w.astype(jnp.bfloat16), 'fsdp', scatter_dimens...  68.9 us
    reduce_scatter x1, waiting for transfers between devices, shards(): lax.psum_scatter(grad_value_w.astype(jnp.bfloat16), 'fsdp', scatter_dimen...  62.3 us
    reduce_scatter x1, waiting for transfers between devices, shards(): lax.psum_scatter(grad_key_w.astype(jnp.bfloat16), 'fsdp', scatter_dimensi...  61.5 us
    unnamed x2, blocking collectives  42.9 us
    all_gather x1, blocking collectives, shards(): lax.all_gather(w_output, 'fsdp', axis=0, tiled=True)  33.6 us
  transfers between devices with their start and end apart: 12, of which 9 were waited for; matrix products, arithmetic and copies ran while one was open for 5% of the time, Pallas kernels for 0%

profile of v1, /device:TPU:0, one launch (start us, length us, event | category | flops | bytes accessed | tf_op | source)
XLA Modules:
  0.0 728.2 jit_solution(17942261707282635411)
XLA Ops:
  9.5 33.3 %all_gather.48 = bf16[576,192]{1,0:T(8,128)(2,1)S(1)} all-gather(bf16[72,192]{1,0:T(8,128)(2,1)} %param.24), channel_id=1, replica_groups=mesh['fsdp'=8,'ctx'=4] {'fsdp'}, dimensions={0}, use_global_device_ids=true | all-gather | bytes 248832 | tf_op jit(solution)/shard_map/all_gather | solution.py:102
  46.5 21.5 %all-reduce.7 = (bf16[576]{0:T(1024)(128)(2,1)S(1)}, bf16[576]{0:T(1024)(128)(2,1)S(1)}) all-reduce(bf16[576]{0:T(1024)(128)(2,1)S(1)} %dynamic-update-slice, bf16[576]{0:T(1024)(128)(2,1)S(1)} %dynamic-update-slice.1), channel_id=1, replica_groups=mesh['fsdp'=8,'ctx'=4] {'fsdp'}, use_global_device_ids=true, to_apply=%add | all-reduce | flops 1152 | bytes 4608
  68.1 31.7 %all_gather.47 = bf16[576,192]{1,0:T(8,128)(2,1)S(1)} all-gather(bf16[72,192]{1,0:T(8,128)(2,1)S(1)} %copy-done.34), channel_id=1, replica_groups=mesh['fsdp'=8,'ctx'=4] {'fsdp'}, dimensions={0}, use_global_device_ids=true | all-gather | bytes 248832 | tf_op jit(solution)/shard_map/all_gather | solution.py:101
  101.0 6.5 all_gather.49
  107.5 32.9 %all_gather.50 = bf16[576,576]{1,0:T(8,128)(2,1)S(1)} all-gather(bf16[72,576]{1,0:T(8,128)(2,1)S(1)} %copy-done.32), channel_id=1, replica_groups=mesh['fsdp'=8,'ctx'=4] {'fsdp'}, dimensions={0}, use_global_device_ids=true | all-gather | bytes 746496 | tf_op jit(solution)/shard_map/all_gather | solution.py:100
  144.6 33.6 %all_gather.51 = bf16[576,576]{1,0:T(8,128)(2,1)S(1)} all-gather(bf16[72,576]{1,0:T(8,128)(2,1)S(1)} %copy-done.33), channel_id=1, replica_groups=mesh['fsdp'=8,'ctx'=4] {'fsdp'}, dimensions={0}, use_global_device_ids=true | all-gather | bytes 746496 | tf_op jit(solution)/shard_map/all_gather | solution.py:103
  178.9 2.9 fusion.90
  181.8 2.9 fusion.91
  184.7 3.8 multiply_convert_fusion
  192.0 8.0 %while.52 = (s32[]{:T(128)}, bf16[2,256,384]{2,1,0:T(8,128)(2,1)}, s32[2]{0:T(128)S(1)}, s32[512]{0:T(512)S(1)}, s32[128]{0:T(128)S(1)}, /*index=5*/bf16[512,384...) while((s32[]{:T(128)}, bf16[2,256,384]{2,1,0:T(8,128)(2,1)}, ...), condition=%wide.region_12.13_spmd, body=%wide.region_11.12_spmd.sunk | while | flops 153780224 | bytes 9319203 | solution.py:262
  200.1 2.3 convolution_convert_fusion.3
  210.2 8.0 %reduce-scatter.25.cloned.1.call-done = bf16[128,384]{1,0:T(8,128)(2,1)} async-done(((bf16[512,384]{1,0:T(8,128)(2,1)}), bf16[128,384]{1,0:T(8,128)(2,1)}) %reduce-scatter.25.cloned.1.call-update) | async-done | bytes 98320
  220.5 2.4 while.55
  229.5 21.3 %all-reduce.6 = (bf16[576]{0:T(1024)(128)(2,1)S(1)}, bf16[576]{0:T(1024)(128)(2,1)S(1)}) all-reduce(bf16[576]{0:T(1024)(128)(2,1)S(1)} %get-tuple-element.563, bf16[576]{0:T(1024)(128)(2,1)S(1)} %get-tuple-element.561), channel_id=11, replica_groups=mesh['fsdp'=8,'ctx'=4] {'fsdp'}, use_global_device_ids=true, to_apply=%region_30.31.clone | all-reduce | flops 1152 | bytes 4608
  250.9 31.9 %reduce-scatter.29.cloned.1.call-done = bf16[72,576]{1,0:T(8,128)(2,1)} async-done(((bf16[576,576]{1,0:T(8,128)(2,1)}), bf16[72,576]{1,0:T(8,128)(2,1)}) %reduce-scatter.29.cloned.1.call-update) | async-done | bytes 82960
  282.8 68.9 %reduce-scatter.19.cloned.1.call-done = bf16[72,1536]{1,0:T(8,128)(2,1)} async-done(((bf16[576,1536]{1,0:T(8,128)(2,1)}), bf16[72,1536]{1,0:T(8,128)(2,1)}) %reduce-scatter.19.cloned.1.call-update) | async-done | bytes 221200 | tf_op jit(solution)/shard_map/reduce_scatter | solution.py:301
  351.7 69.0 %reduce-scatter.21.cloned.1.call-done = bf16[72,1536]{1,0:T(8,128)(2,1)} async-done(((bf16[576,1536]{1,0:T(8,128)(2,1)}), bf16[72,1536]{1,0:T(8,128)(2,1)}) %reduce-scatter.21.cloned.1.call-update) | async-done | bytes 221200 | tf_op jit(solution)/shard_map/reduce_scatter | solution.py:304
  420.7 69.8 %reduce-scatter.23.cloned.1.call-done = bf16[192,576]{1,0:T(8,128)(2,1)} async-done(((bf16[1536,576]{1,0:T(8,128)(2,1)}), bf16[192,576]{1,0:T(8,128)(2,1)}) %reduce-scatter.23.cloned.1.call-update) | async-done | bytes 221200 | tf_op jit(solution)/shard_map/reduce_scatter | solution.py:307
  491.3 61.5 %reduce-scatter.15.cloned.1.call-done = bf16[72,192]{1,0:T(8,128)(2,1)} async-done(((bf16[576,192]{1,0:T(8,128)(2,1)}), bf16[72,192]{1,0:T(8,128)(2,1)}) %reduce-scatter.15.cloned.1.call-update) | async-done | bytes 27664 | tf_op jit(solution)/shard_map/reduce_scatter | solution.py:292
  552.8 62.3 %reduce-scatter.17.cloned.1.call-done = bf16[72,192]{1,0:T(8,128)(2,1)} async-done(((bf16[576,192]{1,0:T(8,128)(2,1)}), bf16[72,192]{1,0:T(8,128)(2,1)}) %reduce-scatter.17.cloned.1.call-update) | async-done | bytes 27664 | tf_op jit(solution)/shard_map/reduce_scatter | solution.py:295
  615.1 11.4 %all-reduce.8 = (bf16[72,192]{1,0:T(8,128)(2,1)S(1)}, bf16[72,192]{1,0:T(8,128)(2,1)S(1)}, bf16[72]{0:T(256)(128)(2,1)S(1)}, bf16[72]{0:T(256)(128)(2,1)S(1)}) all-reduce(bf16[72,192]{1,0:T(8,128)(2,1)} %reduce-scatter.15.cloned.1.call-done, ...), channel_id=1, replica_groups=mesh['fsdp'=8,'ctx'=4] {'ctx'}, use_global_device_ids=true, to_apply=%region_18.19 | all-reduce | flops 27792 | bytes 111168 | tf_op jit(solution)/shard_map/psum | solution.py:321
  628.9 50.1 %reduce-scatter.27.cloned.1.call-done = bf16[72,576]{1,0:T(8,128)(2,1)} async-done(((bf16[576,576]{1,0:T(8,128)(2,1)}), bf16[72,576]{1,0:T(8,128)(2,1)}) %reduce-scatter.27.cloned.1.call-update) | async-done | bytes 82960
  679.0 6.5 all-gather
  686.2 29.3 %all-reduce.12.cloned.1.call-done = (bf16[72,576]{1,0:T(8,128)(2,1)}, bf16[72,1536]{1,0:T(8,128)(2,1)}, bf16[72,1536]{1,0:T(8,128)(2,1)}, bf16[192,576]{1,0:T(8,128)(2,1)}) async-done(((bf16[72,576]{1,0:T(8,128)(2,1)}, bf16[72,1536]{1,0:T(8,128)(2,1)}, bf16[72,1536]{1,0:T(8,128)(2,1)}, bf16[192,576]{1,0:T(8,128)(2,1)}), (bf16[72,576]{1,0:T(8,128)(2,1)}, bf16[72,1536]{1,0:T(8,128)(2,1)}, ...) | async-done | bytes 746512 | tf_op jit(solution)/shard_map/psum | solution.py:323
  (224 shorter events, 52.1 us)
Async XLA Ops:
  7.2 60.8 %copy-start = (bf16[1,128,576]{1,2,0:T(8,128)(2,1)S(1)}, bf16[1,128,576]{1,2,0:T(8,128)(2,1)}, u32[]{:S(2)}) copy-start(bf16[1,128,576]{1,2,0:T(8,128)(2,1)} %param.20) | copy-start | bytes 442372
  7.2 60.9 %copy-start.34 = (bf16[72,192]{1,0:T(8,128)(2,1)S(1)}, bf16[72,192]{1,0:T(8,128)(2,1)}, u32[]{:S(2)}) copy-start(bf16[72,192]{1,0:T(8,128)(2,1)} %param.23) | copy-start | bytes 82948
  7.2 171.7 %all-gather.5.cloned.1.call-start = ((), (), s32[]{:S(2)}) async-start(), calls=%async_computation.8 | async-start | bytes 1990656 | tf_op jit(solution)/shard_map/all_gather | solution.py:104
  7.9 173.9 %all-gather.7.cloned.1.call-start = ((), (), s32[]{:S(2)}) async-start(), calls=%async_computation.9 | async-start | bytes 1990656 | tf_op jit(solution)/shard_map/all_gather | solution.py:105
  8.7 176.0 %all-gather.9.cloned.1.call-start = ((), (), s32[]{:S(2)}) async-start(), calls=%async_computation.10 | async-start | bytes 2211840 | tf_op jit(solution)/shard_map/all_gather | solution.py:106
  9.4 208.8 %reduce-scatter.25.cloned.1.call-start = ((), (), s32[]{:S(2)}) async-start(), calls=%async_computation.16 | async-start | bytes 491520
  9.5 91.3 %copy-start.31 = (s32[1,512]{1,0:T(1,128)S(1)}, s32[1,512]{1,0:T(1,128)}, u32[]{:S(2)}) copy-start(s32[1,512]{1,0:T(1,128)} %param.21) | copy-start | bytes 6148
  42.8 58.2 %copy-start.20 = (bf16[576,192]{1,0:T(8,128)(2,1)}, bf16[576,192]{1,0:T(8,128)(2,1)S(1)}, u32[]{:S(2)}) copy-start(bf16[576,192]{1,0:T(8,128)(2,1)S(1)} %all_gather.48) | copy-start | bytes 663556
  99.8 7.6 %copy-start.32 = (bf16[72,576]{1,0:T(8,128)(2,1)S(1)}, bf16[72,576]{1,0:T(8,128)(2,1)}, u32[]{:S(2)}) copy-start(bf16[72,576]{1,0:T(8,128)(2,1)} %param.22) | copy-start | bytes 248836
  144.5 34.1 %copy-start.22 = (f32[128,3,3,64]{0,3,2,1:T(8,128)}, f32[128,3,3,64]{0,3,2,1:T(8,128)S(1)}, u32[]{:S(2)}) copy-start(f32[128,3,3,64]{0,3,2,1:T(8,128)S(1)} %get-tuple-element.451) | copy-start | bytes 884740
  144.6 34.1 %copy-start.18 = (bf16[128,3,3,64]{0,3,2,1:T(8,128)(2,1)}, bf16[128,3,3,64]{0,3,2,1:T(8,128)(2,1)S(1)}, u32[]{:S(2)}) copy-start(bf16[128,3,3,64]{0,3,2,1:T(8,128)(2,1)S(1)} %convert_element_type.229) | copy-start | bytes 442372
  178.7 3.1 copy-start.35
  184.7 3.8 copy-start.1
  192.0 8.1 %copy-start.19 = (bf16[128,3,3,64]{0,3,2,1:T(8,128)(2,1)S(1)}, bf16[128,3,3,64]{0,3,2,1:T(8,128)(2,1)}, u32[]{:S(2)}) copy-start(bf16[128,3,3,64]{0,3,2,1:T(8,128)(2,1)} %copy-done.18) | copy-start | bytes 442372
  200.0 82.8 %reduce-scatter.29.cloned.1.call-start = ((), (), s32[]{:S(2)}) async-start(), calls=%async_computation.18 | async-start | bytes 829440
  202.4 149.3 %reduce-scatter.19.cloned.1.call-start = ((), (), s32[]{:S(2)}) async-start(), calls=%async_computation.13 | async-start | bytes 1990656 | tf_op jit(solution)/shard_map/reduce_scatter | solution.py:301
  204.3 216.3 %reduce-scatter.21.cloned.1.call-start = ((), (), s32[]{:S(2)}) async-start(), calls=%async_computation.14 | async-start | bytes 1990656 | tf_op jit(solution)/shard_map/reduce_scatter | solution.py:304
  207.1 283.4 %reduce-scatter.23.cloned.1.call-start = ((), (), s32[]{:S(2)}) async-start(), calls=%async_computation.15 | async-start | bytes 2211840 | tf_op jit(solution)/shard_map/reduce_scatter | solution.py:307
  210.2 342.7 %reduce-scatter.15.cloned.1.call-start = ((), (), s32[]{:S(2)}) async-start(), calls=%async_computation.11 | async-start | bytes 331776 | tf_op jit(solution)/shard_map/reduce_scatter | solution.py:292
  220.3 394.9 %reduce-scatter.17.cloned.1.call-start = ((), (), s32[]{:S(2)}) async-start(), calls=%async_computation.12 | async-start | bytes 331776 | tf_op jit(solution)/shard_map/reduce_scatter | solution.py:295
  224.0 454.9 %reduce-scatter.27.cloned.1.call-start = ((), (), s32[]{:S(2)}) async-start(), calls=%async_computation.17 | async-start | bytes 829440
  225.6 489.9 %all-reduce.12.cloned.1.call-start = ((), (), s32[]{:S(2)}) async-start(), calls=%async_computation.19 | async-start | bytes 1560576 | tf_op jit(solution)/shard_map/psum | solution.py:323
  229.0 261.6 %copy-start.6 = (f32[128,576]{0,1:T(8,128)S(1)}, f32[128,576]{0,1:T(8,128)}, u32[]{:S(2)}) copy-start(f32[128,576]{0,1:T(8,128)} %copy-done.5) | copy-start | bytes 884740
  715.5 5.1 copy-start.30
  (27 other events, 37.7 us)
Sparse Core Ops, SparseCore 0:
  10.2 49.4 all-gather.4
  61.9 45.7 all-gather.6
  109.9 57.8 all-gather.8
  200.2 18.0 reduce-scatter.24
  221.5 61.3 reduce-scatter.28
  286.1 65.5 reduce-scatter.18
  355.2 65.4 reduce-scatter.20
  424.1 66.3 reduce-scatter.22
  494.4 58.4 reduce-scatter.14
  556.6 58.5 reduce-scatter.16
  618.5 60.4 reduce-scatter.26
  681.4 34.0 all-reduce.11
